TPU v7x, 32 devices: a whole 2x2x4 slice. The times are simulated.
32 devices in a mesh: tm: 4 (over y, x), rows: 8 (over z, core).
Axes of the slice: x: 2, y: 2, z: 4, core: 2. Of those that a mesh axis runs over, the one named last changes fastest.
Arguments:
- latents: bfloat16 [4, 32, 104, 384], P('tm', 'rows')
- row_valid: int32 [32], P('rows'), may hold values from 0 to 1, as said below
- norm_gain: float32 [384], replicated, may hold values from 0.25 to 1.75
- conv_weight: bfloat16 [10368, 384], P('tm'), may hold values from -0.0625 to 0.0625
- attn_gain: float32 [384], replicated, may hold values from 0.25 to 1.75
- w_query: bfloat16 [384, 384], replicated
- w_key: bfloat16 [384, 384], replicated
- w_value: bfloat16 [384, 384], replicated, may hold values from -0.3125 to 0.3125
- w_out: bfloat16 [384, 384], replicated, may hold values from -0.3125 to 0.3125
- cotangent: bfloat16 [4, 32, 104, 384], P('tm', 'rows'), may hold values from -6 to 6
Outputs:
- input_grad: bfloat16 [4, 32, 104, 384], P('tm', 'rows')
- conv_weight_grad: float32 [10368, 384], P(('tm', 'rows'))
- attn_weight_grad: float32 [1536, 384], P(('tm', 'rows'))
Inputs may be any that keep to these rules, and one draw needn't show every extreme that they name: row_valid is 1 on rows 0 to 15 and 0 on row 31; the rows between may be either.
All inputs are finite; a program needn't handle non-finite values.
Results may differ from a plain program's by a relative error of at most 0.01.
Values may be sent and summed in bfloat16 or wider, within the bound.
A program may use at most 192 MiB of HBM per device.

v0:
```python
import functools
import math

import jax
import jax.numpy as jnp
from jax import lax
from jax.experimental import pallas as pl
from jax.experimental.pallas import tpu as pltpu
from jax.sharding import PartitionSpec as P

epsilon = 1e-06
MESH = pl.DeviceIdType.MESH
ANY = pl.BlockSpec(memory_space=pl.ANY)
IN_VMEM = pl.BlockSpec(memory_space=pltpu.VMEM)
FLAG_ROWS = 16


def contract_last(first_op, second_op):
    return lax.dot_general(
        first_op, second_op, (((1,), (1,)), ((), ())), preferred_element_type=jnp.float32
    )


def contract_first(first_op, second_op):
    return lax.dot_general(
        first_op, second_op, (((0,), (0,)), ((), ())), preferred_element_type=jnp.float32
    )


def dot(first_op, second_op):
    return jnp.dot(first_op, second_op, preferred_element_type=jnp.float32)


def silu_slope(inputs):
    logistic = jax.nn.sigmoid(inputs)
    return logistic * (1.0 + inputs * (1.0 - logistic))


def params(collective_id):
    return pltpu.CompilerParams(
        collective_id=collective_id, has_side_effects=True, vmem_limit_bytes=40 * 1024 * 1024
    )


def signal(barrier, tm_at, row_at):
    pl.semaphore_signal(barrier, inc=1, device_id=(tm_at, row_at), device_id_type=MESH)


def remote(src, dst, send_sem, recv_sem, tm_at, row_at):
    return pltpu.make_async_remote_copy(
        src_ref=src,
        dst_ref=dst,
        send_sem=send_sem,
        recv_sem=recv_sem,
        device_id=(tm_at, row_at),
        device_id_type=MESH,
    )


def slabs_kernel(frames, slabs, x, o, local_sem, send_sem, recv_sem):
    t, r = lax.axis_index("tm"), lax.axis_index("rows")
    rows = x.shape[0]
    has_above, has_below = r > 0, r < slabs - 1
    others = [lax.rem(t + d, frames) for d in range(frames)]
    barrier = pltpu.get_barrier_semaphore()
    for d in range(1, frames):
        signal(barrier, others[d], r)

    @pl.when(has_above)
    def _():
        for d in range(frames):
            signal(barrier, others[d], r - 1)

    @pl.when(has_below)
    def _():
        for d in range(frames):
            signal(barrier, others[d], r + 1)

    sides = has_above.astype(jnp.int32) + has_below.astype(jnp.int32)
    pl.semaphore_wait(barrier, frames - 1 + frames * sides)

    own = pltpu.make_async_copy(x, o.at[t, pl.ds(1, rows)], local_sem)
    own.start()
    slab = [
        remote(x, o.at[t, pl.ds(1, rows)], send_sem.at[d], recv_sem.at[d], others[d], r)
        for d in range(1, frames)
    ]
    down = [
        remote(
            x.at[rows - 1],
            o.at[t, 0],
            send_sem.at[frames + d],
            recv_sem.at[frames + d],
            others[d],
            r + 1,
        )
        for d in range(frames)
    ]
    up = [
        remote(
            x.at[0],
            o.at[t, rows + 1],
            send_sem.at[2 * frames + d],
            recv_sem.at[2 * frames + d],
            others[d],
            r - 1,
        )
        for d in range(frames)
    ]

    @pl.when(has_below)
    def _():
        for copy in down:
            copy.start()

    @pl.when(has_above)
    def _():
        for copy in up:
            copy.start()

    for copy in slab:
        copy.start()
    own.wait()
    for copy in slab:
        copy.wait()

    @pl.when(has_below)
    def _():
        for copy in down:
            copy.wait_send()
        for copy in up:
            copy.wait_recv()

    @pl.when(has_above)
    def _():
        for copy in up:
            copy.wait_send()
        for copy in down:
            copy.wait_recv()


def gather_slabs(block, collective_id):
    frames, slabs = lax.axis_size("tm"), lax.axis_size("rows")
    rows, cols, channels = block.shape
    result = pl.pallas_call(
        functools.partial(slabs_kernel, frames, slabs),
        out_shape=jax.ShapeDtypeStruct((frames, rows + 2, cols, channels), block.dtype),
        in_specs=[ANY],
        out_specs=ANY,
        scratch_shapes=[
            pltpu.SemaphoreType.DMA,
            pltpu.SemaphoreType.DMA((3 * frames,)),
            pltpu.SemaphoreType.DMA((3 * frames,)),
        ],
        compiler_params=params(collective_id),
    )(block)
    r = lax.axis_index("rows")
    row_at = lax.broadcasted_iota(jnp.int32, (1, rows + 2, 1, 1), 1)
    inside = ((row_at > 0) | (r > 0)) & ((row_at < rows + 1) | (r < slabs - 1))
    return jnp.where(inside, result, jnp.zeros((), block.dtype))


def swap_kernel(frames, count, *refs):
    xs, os = refs[:count], refs[count : 2 * count]
    local_sem, send_sem, recv_sem = refs[2 * count :]
    t, r = lax.axis_index("tm"), lax.axis_index("rows")
    others = [lax.rem(t + d, frames) for d in range(frames)]
    barrier = pltpu.get_barrier_semaphore()
    for d in range(1, frames):
        signal(barrier, others[d], r)
    pl.semaphore_wait(barrier, frames - 1)
    copies = []
    for i, (x, o) in enumerate(zip(xs, os)):
        for d in range(1, frames):
            copies.append(
                remote(
                    x.at[others[d]], o.at[t], send_sem.at[i, d], recv_sem.at[i, d], others[d], r
                )
            )
        copies.append(pltpu.make_async_copy(x.at[t], o.at[t], local_sem.at[i]))
    for copy in copies:
        copy.start()
    for copy in copies:
        copy.wait()


def swap_over_tm(arrays, collective_id):
    frames, count = lax.axis_size("tm"), len(arrays)
    return pl.pallas_call(
        functools.partial(swap_kernel, frames, count),
        out_shape=[jax.ShapeDtypeStruct(a.shape, a.dtype) for a in arrays],
        in_specs=[ANY] * count,
        out_specs=[ANY] * count,
        scratch_shapes=[
            pltpu.SemaphoreType.DMA((count,)),
            pltpu.SemaphoreType.DMA((count, frames)),
            pltpu.SemaphoreType.DMA((count, frames)),
        ],
        compiler_params=params(collective_id),
    )(*arrays)


def line_kernel(pairs, x, o, local_sem, send_sem, recv_sem):
    t, r = lax.axis_index("tm"), lax.axis_index("rows")
    q, c = lax.div(r, 2), lax.rem(r, 2)
    sibling = 2 * q + 1 - c
    has_left, has_right = q > 0, q < pairs - 1
    barrier = pltpu.get_barrier_semaphore()
    signal(barrier, t, sibling)

    @pl.when(has_left)
    def _():
        signal(barrier, t, r - 2)

    @pl.when(has_right)
    def _():
        signal(barrier, t, r + 2)

    pl.semaphore_wait(barrier, 1 + has_left.astype(jnp.int32) + has_right.astype(jnp.int32))

    own = pltpu.make_async_copy(x, o.at[r], local_sem)
    own.start()
    to_sibling = remote(x, o.at[r], send_sem.at[0, 0], recv_sem.at[0, 0], t, sibling)

    def held(step, side):
        return r - side * 2 * step

    def hop(step, side):
        at = held(step - 1, side)
        return remote(
            x if step == 1 else o.at[at],
            o.at[at],
            send_sem.at[1 if side > 0 else 2, step],
            recv_sem.at[1 if side > 0 else 2, step],
            t,
            r + 2 * side,
        )

    def hand(step, side):
        at = held(step, side)
        return remote(
            o.at[at],
            o.at[at],
            send_sem.at[3 if side > 0 else 4, step],
            recv_sem.at[3 if side > 0 else 4, step],
            t,
            sibling,
        )

    def arrives(step, side):
        return q - step >= 0 if side > 0 else q + step < pairs

    def sends(step, side):
        onward = has_right if side > 0 else has_left
        return onward if step == 1 else jnp.logical_and(onward, arrives(step - 1, side))

    for side in (1, -1):

        @pl.when(sends(1, side))
        def _():
            hop(1, side).start()

    to_sibling.start()
    for step in range(1, pairs):
        for side in (1, -1):

            @pl.when(arrives(step, side))
            def _():
                hop(step, side).wait_recv()

            if step < pairs - 1:

                @pl.when(sends(step + 1, side))
                def _():
                    hop(step + 1, side).start()

            @pl.when(arrives(step, side))
            def _():
                hand(step, side).start()

    own.wait()
    to_sibling.wait()
    for step in range(1, pairs):
        for side in (1, -1):

            @pl.when(sends(step, side))
            def _():
                hop(step, side).wait_send()

            @pl.when(arrives(step, side))
            def _():
                hand(step, side).wait()


def gather_rows(block, collective_id):
    slabs = lax.axis_size("rows")
    pairs = slabs // 2
    return pl.pallas_call(
        functools.partial(line_kernel, pairs),
        out_shape=jax.ShapeDtypeStruct((slabs,) + block.shape, block.dtype),
        in_specs=[ANY],
        out_specs=ANY,
        scratch_shapes=[
            pltpu.SemaphoreType.DMA,
            pltpu.SemaphoreType.DMA((5, pairs)),
            pltpu.SemaphoreType.DMA((5, pairs)),
        ],
        compiler_params=params(collective_id),
    )(block)


def sum_kernel(pairs, count, *refs):
    gs, os = refs[:count], refs[count : 2 * count]
    near, ready, far = (refs[(2 + i) * count : (3 + i) * count] for i in range(3))
    send_sem, recv_sem, far_send, far_recv = refs[5 * count :]
    t, r = lax.axis_index("tm"), lax.axis_index("rows")
    q, c = lax.div(r, 2), lax.rem(r, 2)
    sibling = 2 * q + 1 - c
    pair_at = [lax.rem(q + d, pairs) for d in range(pairs)]
    barrier = pltpu.get_barrier_semaphore()
    signal(barrier, t, sibling)
    for d in range(1, pairs):
        signal(barrier, t, 2 * pair_at[d] + c)
    pl.semaphore_wait(barrier, pairs)
    order = list(range(1, pairs)) + [0]
    near_copies, far_copies = {}, {}
    for d in order:
        for i in range(count):
            copy = remote(
                gs[i].at[2 * pair_at[d] + 1 - c],
                near[i].at[d],
                send_sem.at[i, d],
                recv_sem.at[i, d],
                t,
                sibling,
            )
            copy.start()
            near_copies[i, d] = copy
    for d in order:
        for i in range(count):
            near_copies[i, d].wait_recv()
            total = gs[i][2 * pair_at[d] + c].astype(jnp.float32) + near[i][d].astype(jnp.float32)
            if d == 0:
                os[i][...] = total
            else:
                ready[i][d] = total.astype(jnp.bfloat16)
                copy = remote(
                    ready[i].at[d],
                    far[i].at[d],
                    far_send.at[i, d],
                    far_recv.at[i, d],
                    t,
                    2 * pair_at[d] + c,
                )
                copy.start()
                far_copies[i, d] = copy
    for d in range(1, pairs):
        for i in range(count):
            far_copies[i, d].wait_recv()
            os[i][...] += far[i][d].astype(jnp.float32)
    for copy in list(near_copies.values()) + list(far_copies.values()):
        copy.wait_send()


def sum_over_rows(arrays, collective_id):
    slabs, count = lax.axis_size("rows"), len(arrays)
    pairs = slabs // 2
    slots = [pltpu.VMEM((pairs,) + a.shape[1:], jnp.bfloat16) for a in arrays]
    return pl.pallas_call(
        functools.partial(sum_kernel, pairs, count),
        out_shape=[jax.ShapeDtypeStruct(a.shape[1:], jnp.float32) for a in arrays],
        in_specs=[IN_VMEM] * count,
        out_specs=[IN_VMEM] * count,
        scratch_shapes=slots * 3 + [pltpu.SemaphoreType.DMA((count, pairs))] * 4,
        compiler_params=params(collective_id),
    )(*arrays)


def column_shifts(slabs, before, after):
    cols = slabs.shape[2]
    width = -(-cols // 16) * 16
    spare = width - cols
    edges = ((before, after), (0, 0))
    return jnp.stack(
        [jnp.pad(slabs, edges + ((1, spare - 1), (0, 0)))]
        + [jnp.pad(slabs, edges + ((0, spare), (0, 0)))]
        + [jnp.pad(slabs[:, :, 1:], edges + ((0, spare + 1), (0, 0)))]
    )


def taps_kernel(rows, cols, transposed, taps, shifted, weight, out, columns):
    f = pl.program_id(0)
    width, channels = shifted.shape[3:]
    count = taps.shape[0]
    total = None
    for j in range(count):
        window = shifted[taps[j, 2], taps[j, 0] + f, pl.ds(taps[j, 1], rows)]
        window = window.reshape(rows * width, channels)
        columns[:, j * channels : (j + 1) * channels] = window
        if transposed:
            term = contract_last(window, weight[j * channels : (j + 1) * channels, :])
            total = term if total is None else total + term
    if not transposed:
        total = dot(columns[...], weight[...])
    total = total.astype(out.dtype).reshape(rows, width, channels)
    out[0] = total[:, :cols]


def sum_taps(shifted, taps, weight, rows, cols, transposed):
    frames = shifted.shape[1] - 2
    width, channels = shifted.shape[3:]
    count = taps.shape[0]
    out = jax.ShapeDtypeStruct((frames, rows, cols, channels), jnp.bfloat16)
    out_spec = pl.BlockSpec((1, rows, cols, channels), lambda f: (f, 0, 0, 0))
    block = (rows * width, count * channels)
    columns = jax.ShapeDtypeStruct((frames * block[0], block[1]), jnp.bfloat16)
    columns_spec = pl.BlockSpec(block, lambda f: (f, 0))
    flops = 2 * frames * block[0] * block[1] * channels
    return pl.pallas_call(
        functools.partial(taps_kernel, rows, cols, transposed),
        grid=(frames,),
        out_shape=out if transposed else (out, columns),
        in_specs=[pl.BlockSpec(memory_space=pltpu.SMEM), IN_VMEM, IN_VMEM],
        out_specs=out_spec if transposed else (out_spec, columns_spec),
        scratch_shapes=[pltpu.VMEM(block, jnp.bfloat16)] if transposed else [],
        cost_estimate=pl.CostEstimate(flops=flops, bytes_accessed=20_000_000, transcendentals=0),
        compiler_params=pltpu.CompilerParams(vmem_limit_bytes=48 * 1024 * 1024),
    )(taps, shifted, weight)


def per_device(
    latents, row_valid, norm_gain, conv_weight, attn_gain, w_query, w_key, w_value, w_out, cotangent
):
    bf16 = jnp.bfloat16
    shape_all = latents.shape
    rows_dev, col_count, channels = shape_all[1:]
    slab_size = rows_dev * col_count
    frames, slabs = lax.axis_size("tm"), lax.axis_size("rows")
    t = lax.axis_index("tm")
    grad_scale = 1.0 / math.sqrt(frames * slabs * slab_size)
    inv_root = 1.0 / math.sqrt(channels)

    own_rows = conv_weight.shape[0]
    tap_total = own_rows * frames // channels
    tap_count = max(
        -(-((i * own_rows) % channels + own_rows) // channels) for i in range(frames)
    )
    first_tap = lax.div(t * own_rows, channels)
    weight_from = t * own_rows - first_tap * channels
    own_weight = lax.dynamic_update_slice(
        jnp.zeros((tap_count * channels, channels), bf16), conv_weight, (weight_from, 0)
    )
    k = jnp.minimum(first_tap + jnp.arange(tap_count, dtype=jnp.int32), tap_total - 1)
    taps = jnp.stack([k // 9, k % 9 // 3, k % 3], axis=1)

    cell_factor = jnp.repeat(row_valid.astype(jnp.float32), col_count)[:, None]
    live_cells = cell_factor > 0
    inputs = latents.reshape(slab_size, channels).astype(jnp.float32)
    first_scale = lax.rsqrt(jnp.mean(inputs * inputs, axis=1, keepdims=True) + epsilon)
    normed_one = inputs * first_scale
    gated_in = normed_one * norm_gain
    conv_in = (jax.nn.silu(gated_in) * cell_factor).astype(bf16)

    grad_out = jnp.where(live_cells, cotangent.reshape(slab_size, channels), jnp.zeros((), bf16))

    history = gather_slabs(conv_in.reshape(rows_dev, col_count, channels), 0)
    conv_terms, columns = sum_taps(
        column_shifts(history, 2, 0), taps, own_weight, rows_dev, col_count, False
    )
    conv_terms = conv_terms.reshape(frames, slab_size, channels)
    (conv_terms,) = swap_over_tm([conv_terms], 1)
    conv_out = jnp.sum(conv_terms.astype(jnp.float32), axis=0)

    mixed_f = (inputs + conv_out).astype(bf16).astype(jnp.float32)
    second_scale = lax.rsqrt(jnp.mean(mixed_f * mixed_f, axis=1, keepdims=True) + epsilon)
    normed_two = mixed_f * second_scale
    attn_in = (normed_two * attn_gain).astype(bf16)

    flag_rows = jnp.pad(row_valid.astype(bf16), (0, FLAG_ROWS - rows_dev))
    flag_rows = jnp.broadcast_to(flag_rows[:, None], (FLAG_ROWS, channels))
    block_size = slab_size + FLAG_ROWS
    gathered = gather_rows(jnp.concatenate([attn_in, flag_rows], axis=0), 2)
    flags_all = jnp.repeat(gathered[:, slab_size : slab_size + rows_dev, 0], col_count, axis=1)
    flags_all = jnp.pad(flags_all, ((0, 0), (0, FLAG_ROWS))).reshape(1, slabs * block_size)
    cells = gathered.reshape(slabs * block_size, channels)

    queries = dot(attn_in, w_query).astype(bf16)
    key_side = contract_last(queries, w_key).astype(bf16)
    d_attended = contract_last(grad_out, w_out).astype(bf16)
    value_side = contract_last(d_attended, w_value).astype(bf16)

    scores = contract_last(key_side, cells) * inv_root
    scores = jnp.where(flags_all > 0, scores, -jnp.inf)
    row_max = jnp.max(scores, axis=1, keepdims=True)
    exponent = jnp.exp(scores - row_max)
    row_total = jnp.sum(exponent, axis=1, keepdims=True)
    weights = exponent / row_total
    weights_b = weights.astype(bf16)
    weighted = dot(weights_b, cells)
    weighted_b = weighted.astype(bf16)
    attended = dot(weighted_b, w_value).astype(bf16)
    d_weights = contract_last(value_side, cells)
    row_delta = jnp.sum(value_side.astype(jnp.float32) * weighted, axis=1, keepdims=True)
    d_scores = (weights * (d_weights - row_delta) * inv_root).astype(bf16)
    d_cells = dot(d_scores, cells).astype(bf16)
    d_query = dot(d_cells, w_key).astype(bf16)
    key_terms = contract_first(
        jnp.concatenate([d_scores, weights_b], axis=0),
        jnp.concatenate([key_side, value_side], axis=0),
    ).astype(bf16)
    grad_stack = (
        jnp.concatenate(
            [
                contract_first(attn_in, d_query),
                contract_first(d_cells, queries),
                contract_first(weighted_b, d_attended),
                contract_first(attended, grad_out),
            ],
            axis=0,
        )
        * grad_scale
    ).astype(bf16)
    stack_rows = grad_stack.shape[0] // (frames * slabs)
    grad_stack = (
        grad_stack.reshape(frames, slabs, stack_rows, channels)
        .transpose(1, 0, 2, 3)
        .reshape(slabs * frames * stack_rows, channels)
    )
    stack_terms = lax.psum_scatter(grad_stack, "rows", scatter_dimension=0, tiled=True)
    (d_attn_in,) = sum_over_rows([key_terms.reshape(slabs, block_size, channels)], 3)
    d_normed = contract_last(d_query, w_query) + d_attn_in[:slab_size]
    scaled_two = attn_gain * d_normed
    d_mixed = grad_out.astype(jnp.float32) + second_scale * (
        scaled_two - normed_two * jnp.mean(scaled_two * normed_two, axis=1, keepdims=True)
    )
    d_conv = d_mixed.astype(bf16)

    spread = gather_slabs(d_conv.reshape(rows_dev, col_count, channels), 4)
    spare = columns.shape[0] // (frames * rows_dev) - col_count
    d_conv_all = jnp.pad(spread[:, 1 : 1 + rows_dev], ((0, 0), (0, 0), (0, spare), (0, 0)))
    weight_terms = contract_first(columns, d_conv_all.reshape(-1, channels)) * grad_scale
    weight_terms = lax.dynamic_slice(
        weight_terms.astype(bf16), (weight_from, 0), (own_rows, channels)
    )
    block_rows = own_rows // slabs
    padded_rows = -(-block_rows // 16) * 16
    weight_terms = jnp.pad(
        weight_terms.reshape(slabs, block_rows, channels),
        ((0, 0), (0, padded_rows - block_rows), (0, 0)),
    )
    weight_sums = lax.psum_scatter(
        weight_terms.reshape(slabs * padded_rows, channels), "rows", scatter_dimension=0, tiled=True
    )
    conv_weight_grad = weight_sums[:block_rows].astype(jnp.float32)

    input_terms = sum_taps(
        column_shifts(spread, 0, 2), 2 - taps, own_weight, rows_dev, col_count, True
    )
    input_terms, stack_terms = swap_over_tm(
        [
            input_terms.reshape(frames, slab_size, channels),
            stack_terms.reshape(frames, stack_rows, channels),
        ],
        5,
    )
    attn_weight_grad = jnp.sum(stack_terms.astype(jnp.float32), axis=0)

    d_input = jnp.sum(input_terms.astype(jnp.float32), axis=0) * cell_factor
    scaled_one = norm_gain * d_input * silu_slope(gated_in)
    input_grad = d_mixed + first_scale * (
        scaled_one - normed_one * jnp.mean(scaled_one * normed_one, axis=1, keepdims=True)
    )
    return (input_grad.astype(bf16).reshape(shape_all), conv_weight_grad, attn_weight_grad)


def solution(mesh):
    return jax.shard_map(
        per_device,
        mesh=mesh,
        in_specs=(
            P("tm", "rows", None, None),
            P("rows"),
            P(),
            P("tm", None),
            P(),
            P(),
            P(),
            P(),
            P(),
            P("tm", "rows", None, None),
        ),
        out_specs=(P("tm", "rows", None, None), P(("tm", "rows"), None), P(("tm", "rows"), None)),
        check_vma=False,
    )
```

profile of v0, /device:TPU:16, one launch (start us, length us, event | category | flops | bytes accessed | tf_op | source)
XLA Modules:
  0.0 281.2 jit_solution(4712890535243688483)
XLA Ops:
  10.4 25.4 %shard_map.121 = bf16[4,6,104,384]{3,2,1,0:T(8,128)(2,1)S(1)} custom-call(bf16[4,104,384]{2,1,0:T(8,128)(2,1)S(1)} %fusion.55.x), custom_call_target="tpu_custom_call" | custom-call | tf_op jit(solution)/shard_map/pallas_call | solution.py:145
  36.8 3.5 %pad_bitcast_fusion.5 = (bf16[1,6,6,112,384]{4,3,2,1,0:T(8,128)(2,1)S(1)}, bf16[1,6,6,112,384]{4,3,2,1,0:T(8,128)(2,1)}, bf16[1,6,6,112,384]{4,3,2,1,0:T(8,128)(2,1)}) fusion(bf16[4,6,104,384]{3,2,1,0:T(8,128)(2,1)S(1)} %broadcast_select_fusion.1, bf16[4,6,103,384]{3,2,1,0:T(8,128)(2,1)S(1)} %slice.24), kind=kLoop, calls=%fused_computation.23 | loop fusion | bytes 13105152 | tf_op jit(solution)/shard_map/stack | solution.py:384
  40.3 7.0 %pad_maximum_fusion.shifted = bf16[3,6,6,112,384]{4,3,2,1,0:T(8,128)(2,1)} fusion(bf16[1,6,6,112,384]{4,3,2,1,0:T(8,128)(2,1)} %get-tuple-element.29, bf16[1,6,6,112,384]{4,3,2,1,0:T(8,128)(2,1)} %get-tuple-element.18, bf16[1,6,6,112,384]{4,3,2,1,0:T(8,128)(2,1)S(1)} %get-tuple-element.17), kind=kLoop, calls=%fused_computation | loop fusion | flops 9289728 | bytes 18579456 | tf_op jit(solution)/shard_map/stack | solution.py:384
  49.3 12.4 %shard_map.122 = (bf16[4,4,104,384]{3,2,1,0:T(8,128)(2,1)S(1)}, bf16[1792,3072]{1,0:T(8,128)(2,1)}) custom-call(s32[8,3]{1,0:T(8,128)S(1)} %get-tuple-element.14.taps, bf16[3,6,6,112,384]{4,3,2,1,0:T(8,128)(2,1)} %pad_maximum_fusion.shifted, bf16[3072,384]{1,0:T(8,128)(2,1)S(1)} %constant_dynamic-update-slice_fusion.weight), custom_call_target="tpu_custom_call" | custom-call | flops 4227858432 | bytes 20000000 | tf_op jit(solution)/shard_map/pallas_call | solution.py:419
  61.7 17.5 %shard_map.123 = bf16[4,416,384]{2,1,0:T(8,128)(2,1)S(1)} custom-call(bf16[4,416,384]{2,1,0:T(8,128)(2,1)S(1)} %bitcast.130), custom_call_target="tpu_custom_call" | custom-call | tf_op jit(solution)/shard_map/pallas_call | solution.py:189
  81.4 23.1 %shard_map.124 = bf16[8,432,384]{2,1,0:T(8,128)(2,1)S(1)} custom-call(bf16[432,384]{1,0:T(8,128)(2,1)S(1)} %pad_maximum_fusion.2.x), custom_call_target="tpu_custom_call" | custom-call | tf_op jit(solution)/shard_map/pallas_call | solution.py:298
  107.8 1.9 fusion.77
  112.2 3.0 %fusion.74 = bf16[416,3456]{1,0:T(8,128)(2,1)} fusion(f32[416]{0:T(512)S(1)} %fusion.12, f32[416,3456]{1,0:T(8,128)S(1)} %get-tuple-element.22, f32[416]{0:T(512)S(1)} %get-tuple-element.21), kind=kLoop, calls=%fused_computation.131 | loop fusion | flops 4313088 | bytes 8629504 | tf_op jit(solution)/shard_map/convert_element_type | solution.py:498
  120.0 3.7 %multiply_reduce_fusion.1 = (f32[416]{0:T(512)S(1)}, bf16[416,384]{1,0:T(8,128)(2,1)S(1)}) fusion(bf16[416,384]{1,0:T(8,128)(2,1)S(1)} %convolution_convert_fusion.3, bf16[416,3456]{1,0:T(8,128)(2,1)} %fusion.74, bf16[3456,384]{1,0:T(8,128)(2,1)S(1)} %bitcast.126), kind=kOutput, calls=%fused_computation.88 | convolution fusion | flops 1104789120 | bytes 6170240 | tf_op jit(solution)/shard_map/dot_general | solution.py:31
  123.8 2.6 fusion.7
  129.4 2.5 fusion.16
  135.2 6.5 %fusion.8 = bf16[3456,384]{1,0:T(8,128)(2,1)S(1)} fusion(bf16[416,3456]{1,0:T(8,128)(2,1)} %fusion.74, bf16[416,3456]{1,0:T(8,128)(2,1)} %copy-done.25, bf16[416,384]{1,0:T(8,128)(2,1)S(1)} %copy-done.22, bf16[416,384]{1,0:T(8,128)(2,1)S(1)} %copy-done.20), kind=kOutput, calls=%fused_computation.13 | convolution fusion | flops 2222407680 | bytes 9043968 | tf_op jit(solution)/shard_map/dot_general | solution.py:25
  141.7 44.0 %shard_map.125 = f32[432,384]{1,0:T(8,128)S(1)} custom-call(bf16[8,432,384]{2,1,0:T(8,128)(2,1)S(1)} %bitcast.129), custom_call_target="tpu_custom_call" | custom-call | tf_op jit(solution)/shard_map/pallas_call | solution.py:369
  186.6 27.1 %shard_map.126 = bf16[4,6,104,384]{3,2,1,0:T(8,128)(2,1)S(1)} custom-call(bf16[4,104,384]{2,1,0:T(8,128)(2,1)S(1)} %bitcast.132), custom_call_target="tpu_custom_call" | custom-call | tf_op jit(solution)/shard_map/pallas_call | solution.py:145
  214.2 5.9 %fusion.80 = f32[3072,384]{1,0:T(8,128)S(1)} fusion(bf16[1792,3072]{1,0:T(8,128)(2,1)S(1)} %bitcast.145, bf16[1792,384]{1,0:T(8,128)(2,1)S(1)} %bitcast.141), kind=kOutput, calls=%fused_computation.136 | convolution fusion | flops 4227858432 | bytes 17104896 | tf_op jit(solution)/shard_map/dot_general | solution.py:25
  221.9 2.8 reshape.294
  224.6 3.1 %pad.49 = bf16[8,336,384]{2,1,0:T(8,128)(2,1)} pad(bf16[8,324,384]{2,1,0:T(8,128)(2,1)} %reshape.294, bf16[]{:T(256)} %constant.32.clone.1), padding=0_0x0_12x0_0 | pad | bytes 4055042 | tf_op jit(solution)/shard_map/jit(_pad)/pad | solution.py:547
  227.7 2.1 slice.25
  229.9 1.8 pad_bitcast_fusion
  233.2 4.3 %pad_maximum_fusion.1.shifted = bf16[3,6,6,112,384]{4,3,2,1,0:T(8,128)(2,1)} fusion(bf16[1,6,6,112,384]{4,3,2,1,0:T(8,128)(2,1)S(1)} %pad_bitcast_fusion, bf16[1,6,6,112,384]{4,3,2,1,0:T(8,128)(2,1)S(1)} %get-tuple-element.16, bf16[1,6,6,112,384]{4,3,2,1,0:T(8,128)(2,1)S(1)} %get-tuple-element.15), kind=kLoop, calls=%fused_computation.1 | loop fusion | flops 9289728 | bytes 18579456 | tf_op jit(solution)/shard_map/stack | solution.py:384
  237.5 11.4 %shard_map.127 = bf16[4,4,104,384]{3,2,1,0:T(8,128)(2,1)S(1)} custom-call(s32[8,3]{1,0:T(8,128)S(1)} %get-tuple-element.13.taps, bf16[3,6,6,112,384]{4,3,2,1,0:T(8,128)(2,1)} %pad_maximum_fusion.1.shifted, bf16[3072,384]{1,0:T(8,128)(2,1)S(1)} %copy-done.2), custom_call_target="tpu_custom_call" | custom-call | flops 4227858432 | bytes 20000000 | tf_op jit(solution)/shard_map/pallas_call | solution.py:419
  249.8 19.0 %shard_map.128 = (bf16[4,416,384]{2,1,0:T(8,128)(2,1)S(1)}, bf16[4,48,384]{2,1,0:T(8,128)(2,1)S(1)}) custom-call(bf16[4,416,384]{2,1,0:T(8,128)(2,1)S(1)} %bitcast.131, bf16[4,48,384]{2,1,0:T(8,128)(2,1)S(1)} %bitcast.133), custom_call_target="tpu_custom_call" | custom-call | tf_op jit(solution)/shard_map/pallas_call | solution.py:189
  270.3 2.4 fusion.43
  272.6 1.8 slice_convert_fusion
  (126 shorter events, 31.9 us)
Async XLA Ops:
  7.2 97.8 %copy-start = (bf16[384,384]{1,0:T(8,128)(2,1)S(1)}, bf16[384,384]{1,0:T(8,128)(2,1)}, u32[]{:S(2)}) copy-start(bf16[384,384]{1,0:T(8,128)(2,1)} %param.15) | copy-start | bytes 884740
  7.2 241.7 %reduce-scatter.3.cloned.1.call-start = ((), (), s32[]{:S(2)}) async-start(), calls=%async_computation.2 | async-start | bytes 1327104 | tf_op jit(solution)/shard_map/reduce_scatter | solution.py:529
  49.2 12.5 %copy-start.1 = (bf16[3072,384]{1,0:T(8,128)(2,1)}, bf16[3072,384]{1,0:T(8,128)(2,1)S(1)}, u32[]{:S(2)}) copy-start(bf16[3072,384]{1,0:T(8,128)(2,1)S(1)} %constant_dynamic-update-slice_fusion.weight) | copy-start | bytes 7077892
  61.7 17.7 %copy-start.5 = (bf16[1,4,104,384]{3,2,1,0:T(8,128)(2,1)S(1)}, bf16[1,4,104,384]{3,2,1,0:T(8,128)(2,1)}, u32[]{:S(2)}) copy-start(bf16[1,4,104,384]{3,2,1,0:T(8,128)(2,1)} %param.10) | copy-start | bytes 958468
  61.7 18.0 %copy-start.24 = (f32[384]{0:T(512)S(1)}, f32[384]{0:T(512)}, u32[]{:S(2)}) copy-start(f32[384]{0:T(512)} %param.14) | copy-start | bytes 4612
  107.8 1.9 copy-start.19
  109.7 2.5 copy-start.4
  118.5 5.3 %slice-start = ((s8[5750784]{0:T(1024)(128)(4,1)}), s8[4194304]{0:T(1024)(128)(4,1)S(1)}, s32[]{:S(2)}) async-start(s8[5750784]{0:T(1024)(128)(4,1)} %bitcast.134), calls=%async_computation.4 | async-start | bytes 8388608
  120.0 3.8 %copy-start.21 = (bf16[416,384]{1,0:T(8,128)(2,1)}, bf16[416,384]{1,0:T(8,128)(2,1)S(1)}, u32[]{:S(2)}) copy-start(bf16[416,384]{1,0:T(8,128)(2,1)S(1)} %convolution_convert_fusion.3) | copy-start | bytes 958468
  120.0 3.8 %slice-start.1 = ((s8[5750784]{0:T(1024)(128)(4,1)}), s8[1556480]{0:T(1024)(128)(4,1)S(1)}, s32[]{:S(2)}) async-start(s8[5750784]{0:T(1024)(128)(4,1)} %bitcast.134), calls=%async_computation.5 | async-start | bytes 3112960
  123.7 5.2 %copy-start.16 = (bf16[416,384]{1,0:T(8,128)(2,1)}, bf16[416,384]{1,0:T(8,128)(2,1)S(1)}, u32[]{:S(2)}) copy-start(bf16[416,384]{1,0:T(8,128)(2,1)S(1)} %get-tuple-element.24) | copy-start | bytes 958468
  126.4 2.1 copy-start.13
  128.2 3.7 %copy-start.7 = (bf16[416,384]{1,0:T(8,128)(2,1)S(1)}, bf16[416,384]{1,0:T(8,128)(2,1)}, u32[]{:S(2)}) copy-start(bf16[416,384]{1,0:T(8,128)(2,1)} %copy-done.6) | copy-start | bytes 958468
  132.3 2.8 %copy-start.20 = (bf16[416,384]{1,0:T(8,128)(2,1)S(1)}, bf16[416,384]{1,0:T(8,128)(2,1)}, u32[]{:S(2)}) copy-start(bf16[416,384]{1,0:T(8,128)(2,1)} %copy-done.19) | copy-start | bytes 958468
  132.3 2.8 %copy-start.22 = (bf16[416,384]{1,0:T(8,128)(2,1)S(1)}, bf16[416,384]{1,0:T(8,128)(2,1)}, u32[]{:S(2)}) copy-start(bf16[416,384]{1,0:T(8,128)(2,1)} %copy-done.21) | copy-start | bytes 958468
  134.9 137.8 %reduce-scatter.5.cloned.1.call-start = ((), (), s32[]{:S(2)}) async-start(), calls=%async_computation.3 | async-start | bytes 2322432 | tf_op jit(solution)/shard_map/reduce_scatter | solution.py:551
  135.2 79.0 %slice-start.2 = ((s8[11010048]{0:T(1024)(128)(4,1)}), s8[4194304]{0:T(1024)(128)(4,1)S(1)}, s32[]{:S(2)}) async-start(s8[11010048]{0:T(1024)(128)(4,1)} %bitcast.144), calls=%async_computation.6 | async-start | bytes 8388608
  135.2 79.0 %slice-start.3 = ((s8[11010048]{0:T(1024)(128)(4,1)}), s8[4194304]{0:T(1024)(128)(4,1)S(1)}, s32[]{:S(2)}) async-start(s8[11010048]{0:T(1024)(128)(4,1)} %bitcast.144), calls=%async_computation.7 | async-start | bytes 8388608
  141.7 44.0 %copy-start.8 = (bf16[416,384]{1,0:T(8,128)(2,1)S(1)}, bf16[416,384]{1,0:T(8,128)(2,1)}, u32[]{:S(2)}) copy-start(bf16[416,384]{1,0:T(8,128)(2,1)} %get-tuple-element.12) | copy-start | bytes 958468
  141.7 44.6 %copy-start.14 = (bf16[1,4,104,384]{3,2,1,0:T(8,128)(2,1)S(1)}, bf16[1,4,104,384]{3,2,1,0:T(8,128)(2,1)}, u32[]{:S(2)}) copy-start(bf16[1,4,104,384]{3,2,1,0:T(8,128)(2,1)} %param.19) | copy-start | bytes 958468
  185.7 28.5 %slice-start.4 = ((s8[11010048]{0:T(1024)(128)(4,1)}), s8[2621440]{0:T(1024)(128)(4,1)S(1)}, s32[]{:S(2)}) async-start(s8[11010048]{0:T(1024)(128)(4,1)} %bitcast.144), calls=%async_computation.8 | async-start | bytes 5242880
  233.1 4.3 %copy-start.2 = (bf16[3072,384]{1,0:T(8,128)(2,1)S(1)}, bf16[3072,384]{1,0:T(8,128)(2,1)}, u32[]{:S(2)}) copy-start(bf16[3072,384]{1,0:T(8,128)(2,1)} %copy-done.1) | copy-start | bytes 7077892
  237.5 32.8 %copy-start.9 = (bf16[416,384]{1,0:T(8,128)(2,1)S(1)}, bf16[416,384]{1,0:T(8,128)(2,1)}, u32[]{:S(2)}) copy-start(bf16[416,384]{1,0:T(8,128)(2,1)} %get-tuple-element.12) | copy-start | bytes 958468
  248.8 20.2 %copy-start.23 = (f32[384]{0:T(512)S(1)}, f32[384]{0:T(512)}, u32[]{:S(2)}) copy-start(f32[384]{0:T(512)} %param.12) | copy-start | bytes 4612
  (9 other events, 11.2 us)
Sparse Core Ops, SparseCore 0:
  135.0 50.2 reduce-scatter.2
  227.8 29.0 reduce-scatter.4
where the time goes:
time: 282 us; the launch traced here: 281 us
  Pallas kernels  180 us (64%)
  matrix products  32.5 us (12%)
  other arithmetic  30.2 us (11%)
  local copies, waits for them, and re-layouts  23.7 us (8%)
  between operations  14.8 us (5%)
    pallas_call x2, Pallas kernels, gather_slabs(): pl.pallas_call(functools.partial(slabs_kernel, frames, slabs), out_shape=...  52.5 us
    pallas_call x1, Pallas kernels, sum_over_rows(): pl.pallas_call(functools.partial(sum_kernel, pairs, count), out_shape=[ja...  44 us
    pallas_call x2, Pallas kernels, swap_over_tm(): pl.pallas_call(functools.partial(swap_kernel, frames, count), out_shape=[...  36.5 us
    pallas_call x2, Pallas kernels, sum_taps(): pl.pallas_call(functools.partial(taps_kernel, rows, cols, transposed), gr...  23.8 us
    pallas_call x1, Pallas kernels, gather_rows(): pl.pallas_call(functools.partial(line_kernel, pairs), out_shape=jax.Shape...  23.1 us
    dot_general x6, matrix products, contract_first(): lax.dot_general(first_op, second_op, (((0,), (0,)), ((), ())), preferred_...  16.1 us
    another operation x2, other arithmetic, column_shifts(): jnp.stack([jnp.pad(slabs, edges + ((1, spare - 1), (0, 0)))] + [jnp.pad(s...  11.3 us
    dot_general x6, matrix products, contract_last(): lax.dot_general(first_op, second_op, (((1,), (1,)), ((), ())), preferred_...  9.32 us
  transfers between devices with their start and end apart: 2, of which 0 were waited for; matrix products, arithmetic and copies ran while one was open for 12% of the time, Pallas kernels for 36%

commit v1 on v0

--- a/solution.py
+++ b/solution.py
@@ -428,6 +428,68 @@
     )(taps, shifted, weight)
 
 
+def attention_kernel(
+    inv_root, cells, bias, key_side, value_side, weighted_out, d_cells_out, terms, exponents, total
+):
+    slabs = cells.shape[0]
+    rows, channels = key_side.shape
+
+    def score(n, row_max):
+        scores = contract_last(key_side[...], cells[n]) * inv_root + bias[n]
+        exponents[n] = scores
+        return jnp.maximum(row_max, jnp.max(scores, axis=1, keepdims=True))
+
+    row_max = lax.fori_loop(0, slabs, score, jnp.full((rows, 1), -jnp.inf, jnp.float32))
+    total[...] = jnp.zeros_like(total)
+
+    def weigh(n, row_total):
+        exponent = jnp.exp(exponents[n] - row_max)
+        exponents[n] = exponent
+        total[...] += dot(exponent.astype(jnp.bfloat16), cells[n])
+        return row_total + jnp.sum(exponent, axis=1, keepdims=True)
+
+    row_total = lax.fori_loop(0, slabs, weigh, jnp.zeros((rows, 1), jnp.float32))
+    inverse = 1.0 / row_total
+    weighted = total[...] * inverse
+    weighted_out[...] = weighted.astype(jnp.bfloat16)
+    row_delta = jnp.sum(value_side[...].astype(jnp.float32) * weighted, axis=1, keepdims=True)
+    total[...] = jnp.zeros_like(total)
+
+    def back(n, carry):
+        d_weights = contract_last(value_side[...], cells[n])
+        weights = exponents[n] * inverse
+        d_scores = (weights * (d_weights - row_delta) * inv_root).astype(jnp.bfloat16)
+        total[...] += dot(d_scores, cells[n])
+        slab_terms = contract_first(d_scores, key_side[...])
+        slab_terms += contract_first(weights.astype(jnp.bfloat16), value_side[...])
+        terms[n] = slab_terms.astype(jnp.bfloat16)
+        return carry
+
+    lax.fori_loop(0, slabs, back, 0)
+    d_cells_out[...] = total[...].astype(jnp.bfloat16)
+
+
+def attention(cells, bias, key_side, value_side):
+    slabs, block_size, channels = cells.shape
+    rows = key_side.shape[0]
+    side = jax.ShapeDtypeStruct((rows, channels), jnp.bfloat16)
+    work = rows * slabs * block_size
+    return pl.pallas_call(
+        functools.partial(attention_kernel, 1.0 / math.sqrt(channels)),
+        out_shape=(side, side, jax.ShapeDtypeStruct(cells.shape, jnp.bfloat16)),
+        in_specs=[IN_VMEM] * 4,
+        out_specs=(IN_VMEM,) * 3,
+        scratch_shapes=[
+            pltpu.VMEM((slabs, rows, block_size), jnp.float32),
+            pltpu.VMEM((rows, channels), jnp.float32),
+        ],
+        cost_estimate=pl.CostEstimate(
+            flops=12 * work * channels, bytes_accessed=8_000_000, transcendentals=work
+        ),
+        compiler_params=pltpu.CompilerParams(vmem_limit_bytes=48 * 1024 * 1024),
+    )(cells, bias, key_side, value_side)
+
+
 def per_device(
     latents, row_valid, norm_gain, conv_weight, attn_gain, w_query, w_key, w_value, w_out, cotangent
 ):
@@ -438,7 +500,6 @@
     frames, slabs = lax.axis_size("tm"), lax.axis_size("rows")
     t = lax.axis_index("tm")
     grad_scale = 1.0 / math.sqrt(frames * slabs * slab_size)
-    inv_root = 1.0 / math.sqrt(channels)
 
     own_rows = conv_weight.shape[0]
     tap_total = own_rows * frames // channels
@@ -481,33 +542,17 @@
     block_size = slab_size + FLAG_ROWS
     gathered = gather_rows(jnp.concatenate([attn_in, flag_rows], axis=0), 2)
     flags_all = jnp.repeat(gathered[:, slab_size : slab_size + rows_dev, 0], col_count, axis=1)
-    flags_all = jnp.pad(flags_all, ((0, 0), (0, FLAG_ROWS))).reshape(1, slabs * block_size)
-    cells = gathered.reshape(slabs * block_size, channels)
+    flags_all = jnp.pad(flags_all, ((0, 0), (0, FLAG_ROWS)))[:, None, :]
+    bias = jnp.where(flags_all > 0, 0.0, -jnp.inf).astype(jnp.float32)
 
     queries = dot(attn_in, w_query).astype(bf16)
     key_side = contract_last(queries, w_key).astype(bf16)
     d_attended = contract_last(grad_out, w_out).astype(bf16)
     value_side = contract_last(d_attended, w_value).astype(bf16)
 
-    scores = contract_last(key_side, cells) * inv_root
-    scores = jnp.where(flags_all > 0, scores, -jnp.inf)
-    row_max = jnp.max(scores, axis=1, keepdims=True)
-    exponent = jnp.exp(scores - row_max)
-    row_total = jnp.sum(exponent, axis=1, keepdims=True)
-    weights = exponent / row_total
-    weights_b = weights.astype(bf16)
-    weighted = dot(weights_b, cells)
-    weighted_b = weighted.astype(bf16)
+    weighted_b, d_cells, key_terms = attention(gathered, bias, key_side, value_side)
     attended = dot(weighted_b, w_value).astype(bf16)
-    d_weights = contract_last(value_side, cells)
-    row_delta = jnp.sum(value_side.astype(jnp.float32) * weighted, axis=1, keepdims=True)
-    d_scores = (weights * (d_weights - row_delta) * inv_root).astype(bf16)
-    d_cells = dot(d_scores, cells).astype(bf16)
     d_query = dot(d_cells, w_key).astype(bf16)
-    key_terms = contract_first(
-        jnp.concatenate([d_scores, weights_b], axis=0),
-        jnp.concatenate([key_side, value_side], axis=0),
-    ).astype(bf16)
     grad_stack = (
         jnp.concatenate(
             [
@@ -527,7 +572,7 @@
         .reshape(slabs * frames * stack_rows, channels)
     )
     stack_terms = lax.psum_scatter(grad_stack, "rows", scatter_dimension=0, tiled=True)
-    (d_attn_in,) = sum_over_rows([key_terms.reshape(slabs, block_size, channels)], 3)
+    (d_attn_in,) = sum_over_rows([key_terms], 3)
     d_normed = contract_last(d_query, w_query) + d_attn_in[:slab_size]
     scaled_two = attn_gain * d_normed
     d_mixed = grad_out.astype(jnp.float32) + second_scale * (

time: 282 us -> 283 us (level)
  Pallas kernels: 180 us -> 200 us
  matrix products: 32.5 us -> 16.9 us
  other arithmetic: 30.2 us -> 26.3 us
    pallas_call x0 -> x1, Pallas kernels: none -> 18.7 us  [attention(): pl.pallas_call(functools.partial(attention_kernel, 1.0 / math.sqrt(channe...]
    dot_general x4 -> x2, matrix products: 7.07 us -> 1.49 us  [dot(): return jnp.dot(first_op, second_op, preferred_element_type=jnp.float32)]
    dot_general x6 -> x4, matrix products: 9.32 us -> 3.79 us  [contract_last(): lax.dot_general(first_op, second_op, (((1,), (1,)), ((), ())), preferred_...]
    dot_general x6 -> x5, matrix products: 16.1 us -> 11.6 us  [contract_first(): lax.dot_general(first_op, second_op, (((0,), (0,)), ((), ())), preferred_...]
    convert_element_type x1 -> x0, other arithmetic: 2.95 us -> none  [per_device(): weights_b = weights.astype(bf16)]
  transfers between devices with their start and end apart: 2 -> 2, of which waited for: 0 -> 0; matrix products, arithmetic and copies ran while one was open for 12% -> 11% of each run, Pallas kernels for 36% -> 37%
where the time goes in v1:
time: 283 us; the launch traced here: 281 us
  Pallas kernels  200 us (71%)
  other arithmetic  26.3 us (9%)
  local copies, waits for them, and re-layouts  22.9 us (8%)
  matrix products  16.9 us (6%)
  between operations  14.6 us (5%)
    pallas_call x2, Pallas kernels, gather_slabs(): pl.pallas_call(functools.partial(slabs_kernel, frames, slabs), out_shape=...  51.8 us
    pallas_call x1, Pallas kernels, sum_over_rows(): pl.pallas_call(functools.partial(sum_kernel, pairs, count), out_shape=[ja...  46.4 us
    pallas_call x2, Pallas kernels, swap_over_tm(): pl.pallas_call(functools.partial(swap_kernel, frames, count), out_shape=[...  36.4 us
    pallas_call x2, Pallas kernels, sum_taps(): pl.pallas_call(functools.partial(taps_kernel, rows, cols, transposed), gr...  23.8 us
    pallas_call x1, Pallas kernels, gather_rows(): pl.pallas_call(functools.partial(line_kernel, pairs), out_shape=jax.Shape...  23.1 us
    pallas_call x1, Pallas kernels, attention(): pl.pallas_call(functools.partial(attention_kernel, 1.0 / math.sqrt(channe...  18.7 us
    dot_general x5, matrix products, contract_first(): lax.dot_general(first_op, second_op, (((0,), (0,)), ((), ())), preferred_...  11.6 us
    another operation x2, other arithmetic, column_shifts(): jnp.stack([jnp.pad(slabs, edges + ((1, spare - 1), (0, 0)))] + [jnp.pad(s...  11.3 us
  transfers between devices with their start and end apart: 2, of which 0 were waited for; matrix products, arithmetic and copies ran while one was open for 11% of the time, Pallas kernels for 37%

profile of v1, /device:TPU:16, one launch (start us, length us, event | category | flops | bytes accessed | tf_op | source)
XLA Modules:
  0.0 281.2 jit_solution(9533743329110915351)
XLA Ops:
  10.4 25.4 %shard_map.121 = bf16[4,6,104,384]{3,2,1,0:T(8,128)(2,1)S(1)} custom-call(bf16[4,104,384]{2,1,0:T(8,128)(2,1)S(1)} %fusion.39.x), custom_call_target="tpu_custom_call" | custom-call | tf_op jit(solution)/shard_map/pallas_call | solution.py:145
  36.8 3.5 %pad_bitcast_fusion.5 = (bf16[1,6,6,112,384]{4,3,2,1,0:T(8,128)(2,1)S(1)}, bf16[1,6,6,112,384]{4,3,2,1,0:T(8,128)(2,1)}, bf16[1,6,6,112,384]{4,3,2,1,0:T(8,128)(2,1)}) fusion(bf16[4,6,104,384]{3,2,1,0:T(8,128)(2,1)S(1)} %broadcast_select_fusion.1, bf16[4,6,103,384]{3,2,1,0:T(8,128)(2,1)S(1)} %slice.24), kind=kLoop, calls=%fused_computation.9 | loop fusion | bytes 13105152 | tf_op jit(solution)/shard_map/stack | solution.py:384
  40.3 6.9 %pad_maximum_fusion.shifted = bf16[3,6,6,112,384]{4,3,2,1,0:T(8,128)(2,1)} fusion(bf16[1,6,6,112,384]{4,3,2,1,0:T(8,128)(2,1)} %get-tuple-element.31, bf16[1,6,6,112,384]{4,3,2,1,0:T(8,128)(2,1)} %get-tuple-element.24, bf16[1,6,6,112,384]{4,3,2,1,0:T(8,128)(2,1)S(1)} %get-tuple-element.23), kind=kLoop, calls=%fused_computation | loop fusion | flops 9289728 | bytes 18579456 | tf_op jit(solution)/shard_map/stack | solution.py:384
  49.3 12.4 %shard_map.122 = (bf16[4,4,104,384]{3,2,1,0:T(8,128)(2,1)S(1)}, bf16[1792,3072]{1,0:T(8,128)(2,1)}) custom-call(s32[8,3]{1,0:T(8,128)S(1)} %get-tuple-element.20.taps, bf16[3,6,6,112,384]{4,3,2,1,0:T(8,128)(2,1)} %pad_maximum_fusion.shifted, bf16[3072,384]{1,0:T(8,128)(2,1)S(1)} %constant_dynamic-update-slice_fusion.weight), custom_call_target="tpu_custom_call" | custom-call | flops 4227858432 | bytes 20000000 | tf_op jit(solution)/shard_map/pallas_call | solution.py:419
  61.7 17.4 %shard_map.123 = bf16[4,416,384]{2,1,0:T(8,128)(2,1)S(1)} custom-call(bf16[4,416,384]{2,1,0:T(8,128)(2,1)S(1)} %bitcast.115), custom_call_target="tpu_custom_call" | custom-call | tf_op jit(solution)/shard_map/pallas_call | solution.py:189
  80.7 23.1 %shard_map.124.cells = bf16[8,432,384]{2,1,0:T(8,128)(2,1)S(1)} custom-call(bf16[432,384]{1,0:T(8,128)(2,1)S(1)} %pad_maximum_fusion.2.x), custom_call_target="tpu_custom_call" | custom-call | tf_op jit(solution)/shard_map/pallas_call | solution.py:298
  105.5 1.5 convolution_convert_fusion.4.key_side
  108.1 1.4 convolution_convert_fusion.3
  110.0 18.7 %shard_map.125 = (bf16[416,384]{1,0:T(8,128)(2,1)S(1)}, bf16[416,384]{1,0:T(8,128)(2,1)S(1)}, bf16[8,432,384]{2,1,0:T(8,128)(2,1)S(1)}) custom-call(bf16[8,432,384]{2,1,0:T(8,128)(2,1)} %copy-done.2, f32[8,1,432]{2,1,0:T(1,128)S(1)} %select_n.76.bias, bf16[416,384]{1,0:T(8,128)(2,1)S(1)} %convolution_convert_fusion.4.key_side, ...), custom_call_target="tpu_custom_call" | custom-call | flops 6624903168 | bytes 8000000 | tf_op jit(solution)/shard_map/pallas_call | solution.py:477
  128.7 1.6 copy-done.3
  131.5 1.6 fusion.3
  137.0 46.4 %shard_map.126 = f32[432,384]{1,0:T(8,128)S(1)} custom-call(bf16[8,432,384]{2,1,0:T(8,128)(2,1)S(1)} %copy-done.4), custom_call_target="tpu_custom_call" | custom-call | tf_op jit(solution)/shard_map/pallas_call | solution.py:369
  184.3 26.4 %shard_map.127 = bf16[4,6,104,384]{3,2,1,0:T(8,128)(2,1)S(1)} custom-call(bf16[4,104,384]{2,1,0:T(8,128)(2,1)S(1)} %bitcast.117), custom_call_target="tpu_custom_call" | custom-call | tf_op jit(solution)/shard_map/pallas_call | solution.py:145
  211.2 8.9 %fusion.58 = f32[3072,384]{1,0:T(8,128)S(1)} fusion(bf16[1792,3072]{1,0:T(8,128)(2,1)} %get-tuple-element.15, bf16[1792,384]{1,0:T(8,128)(2,1)S(1)} %bitcast.124), kind=kOutput, calls=%fused_computation.112 | convolution fusion | flops 4227858432 | bytes 17104896 | tf_op jit(solution)/shard_map/dot_general | solution.py:25
  220.1 1.7 fusion
  221.8 2.8 reshape.275
  224.6 3.1 %pad.49 = bf16[8,336,384]{2,1,0:T(8,128)(2,1)} pad(bf16[8,324,384]{2,1,0:T(8,128)(2,1)} %reshape.275, bf16[]{:T(256)} %constant.35.clone.1), padding=0_0x0_12x0_0 | pad | bytes 4055042 | tf_op jit(solution)/shard_map/jit(_pad)/pad | solution.py:592
  227.7 2.1 slice.25
  229.9 1.8 pad_bitcast_fusion
  233.1 4.3 %pad_maximum_fusion.1.shifted = bf16[3,6,6,112,384]{4,3,2,1,0:T(8,128)(2,1)} fusion(bf16[1,6,6,112,384]{4,3,2,1,0:T(8,128)(2,1)S(1)} %pad_bitcast_fusion, bf16[1,6,6,112,384]{4,3,2,1,0:T(8,128)(2,1)S(1)} %get-tuple-element.22, bf16[1,6,6,112,384]{4,3,2,1,0:T(8,128)(2,1)S(1)} %get-tuple-element.21), kind=kLoop, calls=%fused_computation.1 | loop fusion | flops 9289728 | bytes 18579456 | tf_op jit(solution)/shard_map/stack | solution.py:384
  237.5 11.3 %shard_map.128 = bf16[4,4,104,384]{3,2,1,0:T(8,128)(2,1)S(1)} custom-call(s32[8,3]{1,0:T(8,128)S(1)} %get-tuple-element.19.taps, bf16[3,6,6,112,384]{4,3,2,1,0:T(8,128)(2,1)} %pad_maximum_fusion.1.shifted, bf16[3072,384]{1,0:T(8,128)(2,1)S(1)} %copy-done.6), custom_call_target="tpu_custom_call" | custom-call | flops 4227858432 | bytes 20000000 | tf_op jit(solution)/shard_map/pallas_call | solution.py:419
  249.8 19.0 %shard_map.129 = (bf16[4,416,384]{2,1,0:T(8,128)(2,1)S(1)}, bf16[4,48,384]{2,1,0:T(8,128)(2,1)S(1)}) custom-call(bf16[4,416,384]{2,1,0:T(8,128)(2,1)S(1)} %bitcast.116, bf16[4,48,384]{2,1,0:T(8,128)(2,1)S(1)} %bitcast.118), custom_call_target="tpu_custom_call" | custom-call | tf_op jit(solution)/shard_map/pallas_call | solution.py:189
  270.3 2.4 fusion.27
  272.6 1.8 slice_convert_fusion
  (106 shorter events, 21.1 us)
Async XLA Ops:
  7.2 97.1 %copy-start = (bf16[384,384]{1,0:T(8,128)(2,1)S(1)}, bf16[384,384]{1,0:T(8,128)(2,1)}, u32[]{:S(2)}) copy-start(bf16[384,384]{1,0:T(8,128)(2,1)} %param.15) | copy-start | bytes 884740
  7.2 241.7 %reduce-scatter.3.cloned.1.call-start = ((), (), s32[]{:S(2)}) async-start(), calls=%async_computation.2 | async-start | bytes 1327104 | tf_op jit(solution)/shard_map/reduce_scatter | solution.py:574
  47.3 1.6 copy-start.19
  49.2 12.5 %copy-start.5 = (bf16[3072,384]{1,0:T(8,128)(2,1)}, bf16[3072,384]{1,0:T(8,128)(2,1)S(1)}, u32[]{:S(2)}) copy-start(bf16[3072,384]{1,0:T(8,128)(2,1)S(1)} %constant_dynamic-update-slice_fusion.weight) | copy-start | bytes 7077892
  61.7 17.7 %copy-start.8 = (bf16[1,4,104,384]{3,2,1,0:T(8,128)(2,1)S(1)}, bf16[1,4,104,384]{3,2,1,0:T(8,128)(2,1)}, u32[]{:S(2)}) copy-start(bf16[1,4,104,384]{3,2,1,0:T(8,128)(2,1)} %param.10) | copy-start | bytes 958468
  61.7 18.0 %copy-start.24 = (f32[384]{0:T(512)S(1)}, f32[384]{0:T(512)}, u32[]{:S(2)}) copy-start(f32[384]{0:T(512)} %param.14) | copy-start | bytes 4612
  80.6 26.4 %copy-start.10 = (bf16[416,384]{1,0:T(8,128)(2,1)}, bf16[416,384]{1,0:T(8,128)(2,1)S(1)}, u32[]{:S(2)}) copy-start(bf16[416,384]{1,0:T(8,128)(2,1)S(1)} %get-tuple-element.17) | copy-start | bytes 958468
  103.8 6.2 %copy-start.2 = (bf16[8,432,384]{2,1,0:T(8,128)(2,1)}, bf16[8,432,384]{2,1,0:T(8,128)(2,1)S(1)}, u32[]{:S(2)}) copy-start(bf16[8,432,384]{2,1,0:T(8,128)(2,1)S(1)} %shard_map.124.cells) | copy-start | bytes 7962628
  105.5 4.1 %copy-start.21 = (bf16[384,384]{1,0:T(8,128)(2,1)S(1)}, bf16[384,384]{1,0:T(8,128)(2,1)}, u32[]{:S(2)}) copy-start(bf16[384,384]{1,0:T(8,128)(2,1)} %param.17) | copy-start | bytes 884740
  108.1 1.5 copy-start.13
  110.0 20.4 %copy-start.20 = (bf16[384,384]{1,0:T(8,128)(2,1)S(1)}, bf16[384,384]{1,0:T(8,128)(2,1)}, u32[]{:S(2)}) copy-start(bf16[384,384]{1,0:T(8,128)(2,1)} %param.16) | copy-start | bytes 884740
  110.0 20.7 %copy-start.17 = (bf16[416,384]{1,0:T(8,128)(2,1)S(1)}, bf16[416,384]{1,0:T(8,128)(2,1)}, u32[]{:S(2)}) copy-start(bf16[416,384]{1,0:T(8,128)(2,1)} %convolution_convert_fusion.5) | copy-start | bytes 958468
  128.7 1.6 copy-start.3
  130.4 2.8 copy-start.11
  130.7 2.8 copy-start.15
  134.8 2.2 copy-start.4
  136.0 47.4 %copy-start.12 = (bf16[416,384]{1,0:T(8,128)(2,1)S(1)}, bf16[416,384]{1,0:T(8,128)(2,1)}, u32[]{:S(2)}) copy-start(bf16[416,384]{1,0:T(8,128)(2,1)} %get-tuple-element.18) | copy-start | bytes 958468
  136.1 136.6 %reduce-scatter.5.cloned.1.call-start = ((), (), s32[]{:S(2)}) async-start(), calls=%async_computation.3 | async-start | bytes 2322432 | tf_op jit(solution)/shard_map/reduce_scatter | solution.py:596
  136.3 47.2 %copy-start.16 = (bf16[416,384]{1,0:T(8,128)(2,1)S(1)}, bf16[416,384]{1,0:T(8,128)(2,1)}, u32[]{:S(2)}) copy-start(bf16[416,384]{1,0:T(8,128)(2,1)} %copy-done.15) | copy-start | bytes 958468
  137.0 47.0 %copy-start.18 = (bf16[1,4,104,384]{3,2,1,0:T(8,128)(2,1)S(1)}, bf16[1,4,104,384]{3,2,1,0:T(8,128)(2,1)}, u32[]{:S(2)}) copy-start(bf16[1,4,104,384]{3,2,1,0:T(8,128)(2,1)} %param.19) | copy-start | bytes 958468
  233.1 4.3 %copy-start.6 = (bf16[3072,384]{1,0:T(8,128)(2,1)S(1)}, bf16[3072,384]{1,0:T(8,128)(2,1)}, u32[]{:S(2)}) copy-start(bf16[3072,384]{1,0:T(8,128)(2,1)} %copy-done.5) | copy-start | bytes 7077892
  237.5 31.5 %copy-start.9 = (bf16[1,4,104,384]{3,2,1,0:T(8,128)(2,1)S(1)}, bf16[1,4,104,384]{3,2,1,0:T(8,128)(2,1)}, u32[]{:S(2)}) copy-start(bf16[1,4,104,384]{3,2,1,0:T(8,128)(2,1)} %param.10) | copy-start | bytes 958468
  248.8 20.2 %copy-start.23 = (f32[384]{0:T(512)S(1)}, f32[384]{0:T(512)}, u32[]{:S(2)}) copy-start(f32[384]{0:T(512)} %param.12) | copy-start | bytes 4612
  268.8 5.6 %copy-start.1 = (bf16[384,384]{1,0:T(8,128)(2,1)S(1)}, bf16[384,384]{1,0:T(8,128)(2,1)}, u32[]{:S(2)}) copy-start(bf16[384,384]{1,0:T(8,128)(2,1)} %param.15) | copy-start | bytes 884740
  (3 other events, 3.3 us)
Sparse Core Ops, SparseCore 0:
  136.2 51.7 reduce-scatter.2
  227.8 29.5 reduce-scatter.4
